TPU v7x, 256 devices: a whole 4x4x8 slice. The times are simulated.
256 devices in a mesh: section: 2 (over core), dp: 8 (over y, z_lo), tensor: 16 (over x, z_hi).
Axes of the slice: x: 4, y: 4, z: 8 (z_hi: 4, z_lo: 2; z = z_hi * 2 + z_lo), core: 2. Of those that a mesh axis runs over, the one named last changes fastest.
Arguments:
- residual_parts: bfloat16 [2, 3072, 16384], P('section', 'dp', 'tensor'), may hold values from -120 to 120
- attn_out: bfloat16 [2, 3072, 16384], P('section', 'dp', 'tensor'), may hold values from -6 to 6
- ffn_input: bfloat16 [2, 3072, 53248], P('section', 'dp', 'tensor'), may hold values from -6 to 6
- norm_gain: float32 [2, 16384], P('section', 'tensor'), may hold values from 0.25 to 1.75
- mixing: bfloat16 [2, 52, 52], P('section'), may hold values from -0.875 to 0.875
- blocks: int32 [2, 2], P('section'), may hold values from 0 to 25, as said below
Outputs:
- hess_in: float32 [2, 16384, 1024], P('section', 'tensor', 'dp')
- hess_o: float32 [2, 16384, 1024], P('section', 'tensor', 'dp')
- hess_down: float32 [2, 2048, 2048], P('section', 'tensor', 'dp')
Inputs may be any that keep to these rules, and one draw needn't show every extreme that they name: `blocks`: entry [s, 0] is below 16; entry [s, 1] is below 26. In every draw one layer has entry [s, 0] = 0 and entry [s, 1] = 25.
All inputs are finite; a program needn't handle non-finite values.
Results may differ from a plain program's by a relative error of at most 0.0038.
Values may be sent and summed in bfloat16 or wider, within the bound.
No kernel may reach another device: no remote copies, remote signals or barrier semaphores. Data moves between devices by JAX's collectives and lax.ppermute only.
A program may use at most 64 MiB of HBM per device.

v0:
```python
import math
import jax
import jax.numpy as jnp
from jax import lax
from jax.sharding import Mesh
from jax.sharding import PartitionSpec as P

D = 16384
KB = 52
HBLK = 1024
BLK = 2048
TENSOR = ("tensor_0", "tensor_1")
EPS = 1e-05


def passed_along(x, axis, by):
    devices = lax.axis_size(axis)
    pairs = [(i, i + by) for i in range(devices) if 0 <= i + by < devices]
    return lax.ppermute(x, axis, pairs)


def copy_for_each(x, axis):
    devices = lax.axis_size(axis)
    return lax.all_to_all(jnp.broadcast_to(x[None], (devices, *x.shape)), axis, 0, 0, tiled=True)


def over_copies(x, axis):
    everything = copy_for_each(x, axis)
    return jnp.sum(everything, axis=0)


def broadcast_by_axis(x, axes, root):
    x = jnp.where(lax.axis_index(axes) == root, x, jnp.zeros_like(x))
    for axis in axes:
        x = lax.psum(x, axis)
    return x


def in_blocks(x, dim, devices):
    before, after = (x.shape[:dim], x.shape[dim + 1 :])
    return jnp.moveaxis(x.reshape(*before, devices, -1, *after), dim, 0)


def summed_on_arrival(x, axis, dim):
    tiles = in_blocks(x, dim, lax.axis_size(axis))
    arrived = lax.all_to_all(tiles, axis, split_axis=0, concat_axis=0, tiled=True)
    return arrived.sum(axis=0)


def in_one_piece(arrays, axis, dim, along):
    both = jnp.concatenate(arrays, axis=along)
    out, at, done = (lax.psum_scatter(both, axis, scatter_dimension=dim, tiled=True), 0, [])
    for a in arrays:
        done.append(lax.slice_in_dim(out, at, at + a.shape[along], axis=along))
        at += a.shape[along]
    return tuple(done)


def bit_parity(values):
    total = jnp.zeros_like(values)
    for position in range(16):
        total = total + values // (1 << position) % 2
    return total % 2


def sylvester(order):
    index = jnp.arange(order, dtype=jnp.int32)
    parity = bit_parity(jnp.bitwise_and(index[:, None], index[None, :]))
    return (1 - 2 * parity).astype(jnp.float32)


def gram(left, right):
    return lax.dot_general(
        left, right, (((0,), (0,)), ((), ())), preferred_element_type=jnp.float32
    )


def local(residual_parts, attn_out, ffn_input, norm_gain, mixing, blocks):
    local_d = residual_parts.shape[2]
    local_f = ffn_input.shape[2]
    token_rows = residual_parts.shape[1]
    own_part = residual_parts[0]
    earlier = passed_along(own_part, "section", 1)
    layer_in = earlier.astype(jnp.float32) + own_part.astype(jnp.float32)
    square_total = over_copies(jnp.sum(layer_in * layer_in, axis=1), TENSOR)
    normed = (layer_in * lax.rsqrt(square_total / D + EPS)[:, None] * norm_gain[0][None, :]).astype(
        jnp.bfloat16
    )
    attention = attn_out[0]
    first_col = blocks[0, 0] * HBLK
    norm_list, attn_list = ([], [])
    owner = first_col // local_d + 0
    norm_got = broadcast_by_axis(normed, TENSOR, owner)
    attn_got = broadcast_by_axis(attention, TENSOR, owner)
    norm_list.append(norm_got)
    attn_list.append(attn_got)
    norm_block = norm_list[0]
    attn_block = attn_list[0]
    tensor_count = lax.axis_size(TENSOR)
    member = lax.axis_index(TENSOR)
    a_local = local_f // KB
    order_a = a_local * tensor_count
    cube = ffn_input[0].reshape(token_rows, a_local, KB)
    mixed = jnp.einsum("rak,kc->rac", cube, mixing[0], preferred_element_type=jnp.float32)
    turned = jnp.einsum("rac,ae->rec", mixed, sylvester(a_local), precision=lax.Precision.HIGHEST)
    turned = turned.reshape(token_rows, local_f)
    start = blocks[0, 1] * BLK
    doubled = jnp.concatenate([turned, turned], axis=1)
    window = lax.dynamic_slice_in_dim(doubled, start % local_f, BLK, 1)
    target = (start + jnp.arange(BLK, dtype=jnp.int32)) // local_f
    parity = bit_parity(jnp.bitwise_and(target, member))
    signs = (1 - 2 * parity).astype(jnp.float32) / math.sqrt(order_a)
    term = window * signs[None, :]
    own_cols = summed_on_arrival(term, TENSOR, 1).astype(jnp.bfloat16)
    rotated = lax.all_gather(own_cols, TENSOR, axis=1, tiled=True)
    part_in = gram(normed, norm_block)
    part_o = gram(attention, attn_block)
    part_down = gram(own_cols, rotated)
    summed = (
        *in_one_piece((part_in, part_o), "dp", 1, 0),
        lax.psum_scatter(part_down, "dp", scatter_dimension=1, tiled=True),
    )
    scale = 2.0 / (token_rows * lax.axis_size("dp"))
    hess_in = (scale * summed[0])[None]
    hess_o = (scale * summed[1])[None]
    hess_down = (scale * summed[2])[None]
    return (hess_in, hess_o, hess_down)


def solution(mesh):
    finer = Mesh(
        mesh.devices.reshape(mesh.shape["section"], mesh.shape["dp"], 4, 4),
        ("section", "dp", "tensor_0", "tensor_1"),
    )
    in_specs = (
        P("section", "dp", TENSOR),
        P("section", "dp", TENSOR),
        P("section", "dp", TENSOR),
        P("section", TENSOR),
        P("section", None, None),
        P("section", None),
    )
    out_specs = (P("section", TENSOR, "dp"), P("section", TENSOR, "dp"), P("section", TENSOR, "dp"))
    return jax.shard_map(local, mesh=finer, in_specs=in_specs, out_specs=out_specs, check_vma=False)
```

profile of v0, /device:TPU:1, one launch (start us, length us, event | category | flops | bytes accessed | tf_op | source)
XLA Modules:
  0.0 455.9 jit_solution(6343559055614895578)
XLA Ops:
  8.0 0.0 copy-start
  8.0 1.3 collective-permute-start
  9.3 4.4 copy.20
  13.7 3.4 reshape_squeeze.3
  17.1 0.0 copy-done
  17.1 0.0 copy-start.9
  17.1 3.3 fusion.156
  20.4 0.0 copy-done.9
  20.4 0.6 fusion.253
  21.7 8.3 %fusion.4 = f32[384,64,52]{0,1,2:T(8,128)S(1)} fusion(f32[384,64,52]{0,2,1:T(8,128)} %fusion.156), kind=kOutput, calls=%fused_computation.7 | convolution fusion | flops 982917120 | bytes 10223616 | tf_op jit(solution)/shard_map/rac,ae->rec/dot_general | solution.py:105
  30.0 5.4 %copy.23 = f32[384,64,52]{0,2,1:T(8,128)} copy(f32[384,64,52]{0,1,2:T(8,128)S(1)} %fusion.4) | data formatting | bytes 10223616 | tf_op jit(solution)/shard_map/rac,ae->rec/transpose | solution.py:105
  35.4 0.0 copy-start.1
  35.4 6.4 %reshape.401 = f32[384,3328]{0,1:T(8,128)} reshape(f32[384,64,52]{0,2,1:T(8,128)} %copy.23) | data formatting | bytes 10223616 | tf_op jit(solution)/shard_map/reshape | solution.py:106
  41.7 0.1 fusion.207
  41.9 0.0 collective-permute-done
  41.9 0.0 copy-done.1
  41.9 0.0 copy-start.3
  41.9 0.3 multiply_reduce_fusion
  42.2 0.6 broadcast_in_dim.8
  42.8 11.6 %all-to-all-start = ((f32[16,1,384]{2,1,0:T(1,128)}), f32[16,1,384]{2,1,0:T(1,128)S(1)}, u32[]{:S(2)}, u32[]{:S(2)}) async-start(f32[16,1,384]{2,1,0:T(1,128)} %broadcast_in_dim.8), calls=%async_computation | async-start | bytes 49152 | tf_op jit(solution)/shard_map/all_to_all | solution.py:24
  54.5 4.5 fusion.3
  59.0 0.0 copy-done.3
  59.0 4.3 all-to-all-done
  63.3 0.0 copy-start.8
  63.3 0.0 copy-start.7
  63.3 0.6 copy-done.8
  63.9 4.7 %all-to-all-start.1 = ((f32[16,384,128]{1,2,0:T(8,128)}), f32[16,384,128]{1,2,0:T(8,128)S(1)}, u32[]{:S(2)}, u32[]{:S(2)}) async-start(f32[16,384,128]{1,2,0:T(8,128)} %bitcast.13), calls=%async_computation.2 | async-start | bytes 6291456 | tf_op jit(solution)/shard_map/all_to_all | solution.py:46
  68.6 0.0 all-reduce.7.cloned.1.call-start
  69.3 2.1 bitcast_select_fusion
  71.4 0.8 reduce_sum.28
  72.2 0.0 copy-done.7
  72.2 2.6 broadcast_select_fusion
  74.8 0.0 all-reduce.7.cloned.1.call-update
  74.9 0.0 all-gather.2.cloned.1.call-start
  74.9 62.6 %all-to-all-done.1 = f32[16,384,128]{1,2,0:T(8,128)S(1)} async-done(((f32[16,384,128]{1,2,0:T(8,128)}), f32[16,384,128]{1,2,0:T(8,128)S(1)}, u32[]{:S(2)}, u32[]{:S(2)}) %all-to-all-start.1) | async-done | bytes 3145760 | tf_op jit(solution)/shard_map/all_to_all | solution.py:46
  137.5 0.8 reduce_sum.29
  138.3 0.0 copy-start.5
  138.3 0.0 all-gather.2.cloned.1.call-update
  138.4 0.0 all-reduce.5.cloned.1.call-start
  138.4 15.9 %all-reduce.7.cloned.1.call-done = (bf16[384,1024]{1,0:T(8,128)(2,1)}, bf16[384,1024]{1,0:T(8,128)(2,1)}) async-done(((bf16[384,1024]{1,0:T(8,128)(2,1)}, bf16[384,1024]{1,0:T(8,128)(2,1)}), (bf16[384,1024]{1,0:T(8,128)(2,1)}, bf16[384,1024]{1,0:T(8,128)(2,1)})) %all-reduce.7.cloned.1.call-update) | async-done | bytes 1572880 | tf_op jit(solution)/shard_map/psum | solution.py:35
  154.3 0.0 all-reduce.5.cloned.1.call-update
  154.4 0.0 reduce-scatter.5.cloned.1.call-start
  154.4 56.3 %all-gather.2.cloned.1.call-done = bf16[384,2048]{0,1:T(8,128)(2,1)} async-done(((bf16[384,128]{0,1:T(8,128)(2,1)}), bf16[384,2048]{0,1:T(8,128)(2,1)}) %all-gather.2.cloned.1.call-update) | async-done | bytes 1572880 | tf_op jit(solution)/shard_map/all_gather | solution.py:115
  210.7 3.1 fusion.254
  213.8 0.0 reduce-scatter.5.cloned.1.call-update
  213.8 0.0 reduce-scatter.3.cloned.1.call-start
  213.9 41.1 %all-reduce.5.cloned.1.call-done = (bf16[384,1024]{1,0:T(8,128)(2,1)}, bf16[384,1024]{1,0:T(8,128)(2,1)}) async-done(((bf16[384,1024]{1,0:T(8,128)(2,1)}, bf16[384,1024]{1,0:T(8,128)(2,1)}), (bf16[384,1024]{1,0:T(8,128)(2,1)}, bf16[384,1024]{1,0:T(8,128)(2,1)})) %all-reduce.5.cloned.1.call-update) | async-done | bytes 1572880 | tf_op jit(solution)/shard_map/psum | solution.py:35
  255.0 0.0 copy-done.5
  255.0 0.0 copy-start.2
  255.0 0.0 copy-start.4
  255.0 0.0 copy-start.6
  255.0 2.6 convolution_bitcast_fusion
  257.6 0.0 copy-done.2
  257.6 0.0 copy-done.4
  257.7 0.0 copy-done.6
  257.7 1.4 fusion.252
  259.1 4.1 pad_maximum_fusion
  263.2 0.0 reduce-scatter.3.cloned.1.call-update
  263.2 6.4 %reduce-scatter.5.cloned.1.call-done = f32[128,256]{1,0:T(8,128)} async-done(((f32[128,2048]{1,0:T(8,128)}), f32[128,256]{1,0:T(8,128)}) %reduce-scatter.5.cloned.1.call-update) | async-done | bytes 131088 | tf_op jit(solution)/shard_map/reduce_scatter | solution.py:121
  269.6 1.6 multiply_bitcast_fusion
  271.1 174.9 %reduce-scatter.3.cloned.1.call-done = f32[2048,128]{1,0:T(8,128)} async-done(((f32[2048,1024]{1,0:T(8,128)}), f32[2048,128]{1,0:T(8,128)}) %reduce-scatter.3.cloned.1.call-update) | async-done | bytes 1048592 | tf_op jit(solution)/shard_map/reduce_scatter | solution.py:52
  446.1 2.3 fusion.8
  (1 shorter events, 0.0 us)
Async XLA Ops:
  8.0 9.1 %copy-start = (bf16[1,52,52]{2,1,0:T(8,128)(2,1)S(1)}, bf16[1,52,52]{2,1,0:T(8,128)(2,1)}, u32[]{:S(2)}) copy-start(bf16[1,52,52]{2,1,0:T(8,128)(2,1)} %param.10) | copy-start | bytes 16228
  8.0 33.8 %collective-permute-start = (bf16[384,1024]{1,0:T(8,128)(2,1)}, bf16[384,1024]{1,0:T(8,128)(2,1)S(1)}, u32[]{:S(2)}, u32[]{:S(2)}) collective-permute-start(bf16[384,1024]{1,0:T(8,128)(2,1)} %bitcast.43), channel_id=1, source_target_pairs={{0,128},{1,129},{2,130},{3,131},{4,132},{5,133},{6,134},{7,135},{8... | collective-permute-start | bytes 2359304 | tf_op jit(solution)/shard_map/ppermute | solution.py:19
  17.1 3.3 copy-start.9
  35.4 6.5 %copy-start.1 = (bf16[1,384,1024]{2,1,0:T(8,128)(2,1)S(1)}, bf16[1,384,1024]{2,1,0:T(8,128)(2,1)}, u32[]{:S(2)}) copy-start(bf16[1,384,1024]{2,1,0:T(8,128)(2,1)} %param.6) | copy-start | bytes 2359300
  41.9 17.1 %copy-start.3 = (bf16[384,1024]{1,0:T(8,128)(2,1)}, bf16[384,1024]{1,0:T(8,128)(2,1)S(1)}, u32[]{:S(2)}) copy-start(bf16[384,1024]{1,0:T(8,128)(2,1)S(1)} %collective-permute-done) | copy-start | bytes 2359300
  42.8 20.4 %all-to-all-start = ((f32[16,1,384]{2,1,0:T(1,128)}), f32[16,1,384]{2,1,0:T(1,128)S(1)}, u32[]{:S(2)}, u32[]{:S(2)}) async-start(f32[16,1,384]{2,1,0:T(1,128)} %broadcast_in_dim.8), calls=%async_computation | async-start | bytes 49152 | tf_op jit(solution)/shard_map/all_to_all | solution.py:24
  63.3 0.6 copy-start.8
  63.3 8.9 %copy-start.7 = (f32[1,1024]{1,0:T(1,128)S(1)}, f32[1,1024]{1,0:T(1,128)}, u32[]{:S(2)}) copy-start(f32[1,1024]{1,0:T(1,128)} %param.9) | copy-start | bytes 12292
  63.9 73.6 %all-to-all-start.1 = ((f32[16,384,128]{1,2,0:T(8,128)}), f32[16,384,128]{1,2,0:T(8,128)S(1)}, u32[]{:S(2)}, u32[]{:S(2)}) async-start(f32[16,384,128]{1,2,0:T(8,128)} %bitcast.13), calls=%async_computation.2 | async-start | bytes 6291456 | tf_op jit(solution)/shard_map/all_to_all | solution.py:46
  68.6 85.7 %all-reduce.7.cloned.1.call-start = ((), (), s32[]{:S(2)}) async-start(), calls=%async_computation.8 | async-start | bytes 3145728 | tf_op jit(solution)/shard_map/psum | solution.py:35
  74.9 135.8 %all-gather.2.cloned.1.call-start = ((), (), s32[]{:S(2)}) async-start(), calls=%async_computation.5 | async-start | bytes 1671168 | tf_op jit(solution)/shard_map/all_gather | solution.py:115
  138.3 116.7 %copy-start.5 = (bf16[1,384,1024]{2,1,0:T(8,128)(2,1)S(1)}, bf16[1,384,1024]{2,1,0:T(8,128)(2,1)}, u32[]{:S(2)}) copy-start(bf16[1,384,1024]{2,1,0:T(8,128)(2,1)} %param.7) | copy-start | bytes 2359300
  138.4 116.7 %all-reduce.5.cloned.1.call-start = ((), (), s32[]{:S(2)}) async-start(), calls=%async_computation.7 | async-start | bytes 3145728 | tf_op jit(solution)/shard_map/psum | solution.py:35
  154.4 115.2 %reduce-scatter.5.cloned.1.call-start = ((), (), s32[]{:S(2)}) async-start(), calls=%async_computation.6 | async-start | bytes 1179648 | tf_op jit(solution)/shard_map/reduce_scatter | solution.py:121
  213.8 232.2 %reduce-scatter.3.cloned.1.call-start = ((), (), s32[]{:S(2)}) async-start(), calls=%async_computation.4 | async-start | bytes 9437184 | tf_op jit(solution)/shard_map/reduce_scatter | solution.py:52
  255.0 2.6 copy-start.2
  255.0 2.6 copy-start.4
  255.0 2.6 copy-start.6
Sparse Core Ops, SparseCore 0:
  75.0 79.3 all-reduce.6
  157.0 97.9 all-reduce.4
Sparse Core Ops, SparseCore 1:
  138.4 72.2 all-gather.1
  213.9 55.6 reduce-scatter.4
  272.0 174.0 reduce-scatter.2
where the time goes:
time: 457 us; the launch traced here: 456 us
  waiting for transfers between devices  362 us (79%)
  local copies, waits for them, and re-layouts  21.4 us (5%)
  other arithmetic  19.1 us (4%)
  matrix products  18.8 us (4%)
  starting transfers between devices  17.8 us (4%)
  between operations  17.2 us (4%)
    reduce_scatter x1, waiting for transfers between devices, in_one_piece(): lax.psum_scatter(both, axis, scatter_dimension=dim, tiled=True)  175 us
    all_to_all x1, waiting for transfers between devices, summed_on_arrival(): lax.all_to_all(tiles, axis, split_axis=0, concat_axis=0, tiled=True)  62.6 us
    psum x2, waiting for transfers between devices, broadcast_by_axis(): x = lax.psum(x, axis)  57.1 us
    all_gather x1, waiting for transfers between devices, local(): rotated = lax.all_gather(own_cols, TENSOR, axis=1, tiled=True)  56.3 us
    all_to_all x1, starting transfers between devices, copy_for_each(): lax.all_to_all(jnp.broadcast_to(x[None], (devices, *x.shape)), axis, 0, 0...  11.6 us
  transfers between devices with their start and end apart: 8, of which 7 were waited for; matrix products, arithmetic and copies ran while one was open for 12% of the time, Pallas kernels for 0%

commit v1 on v0

--- a/solution.py
+++ b/solution.py
@@ -112,7 +112,9 @@
     signs = (1 - 2 * parity).astype(jnp.float32) / math.sqrt(order_a)
     term = window * signs[None, :]
     own_cols = summed_on_arrival(term, TENSOR, 1).astype(jnp.bfloat16)
-    rotated = lax.all_gather(own_cols, TENSOR, axis=1, tiled=True)
+    rotated = jnp.concatenate(
+        lax.all_to_all(jnp.stack([own_cols] * lax.axis_size(TENSOR)), TENSOR, 0, 0), axis=1
+    )
     part_in = gram(normed, norm_block)
     part_o = gram(attention, attn_block)
     part_down = gram(own_cols, rotated)

time: 457 us -> 502 us (1.098)
  waiting for transfers between devices: 362 us -> 399 us
  starting transfers between devices: 17.8 us -> 27.5 us
    psum x2, waiting for transfers between devices: 57.1 us -> 160 us  [broadcast_by_axis(): x = lax.psum(x, axis)]
    all_gather x1 -> x0, waiting for transfers between devices: 56.3 us -> none  [local(): rotated = lax.all_gather(own_cols, TENSOR, axis=1, tiled=True)]
    all_to_all x0 -> x1, starting transfers between devices: none -> 9.7 us  [local(): lax.all_to_all(jnp.stack([own_cols] * lax.axis_size(TENSOR)), TENSOR, 0, 0)]
    reduce_scatter x1, waiting for transfers between devices: 6.36 us -> 0.03 us  [local(): lax.psum_scatter(part_down, 'dp', scatter_dimension=1, tiled=True)]
  transfers between devices with their start and end apart: 8 -> 8, of which waited for: 7 -> 5; matrix products, arithmetic and copies ran while one was open for 12% -> 10% of each run, Pallas kernels for 0% -> 0%
where the time goes in v1:
time: 502 us; the launch traced here: 501 us
  waiting for transfers between devices  399 us (79%)
  starting transfers between devices  27.5 us (5%)
  local copies, waits for them, and re-layouts  22.7 us (5%)
  matrix products  17.5 us (3%)
  other arithmetic  17.1 us (3%)
  between operations  17 us (3%)
    reduce_scatter x1, waiting for transfers between devices, in_one_piece(): lax.psum_scatter(both, axis, scatter_dimension=dim, tiled=True)  170 us
    psum x2, waiting for transfers between devices, broadcast_by_axis(): x = lax.psum(x, axis)  160 us
    all_to_all x1, waiting for transfers between devices, summed_on_arrival(): lax.all_to_all(tiles, axis, split_axis=0, concat_axis=0, tiled=True)  64.7 us
    all_to_all x1, starting transfers between devices, copy_for_each(): lax.all_to_all(jnp.broadcast_to(x[None], (devices, *x.shape)), axis, 0, 0...  11.6 us
  transfers between devices with their start and end apart: 8, of which 5 were waited for; matrix products, arithmetic and copies ran while one was open for 10% of the time, Pallas kernels for 0%

profile of v1, /device:TPU:1, one launch (start us, length us, event | category | flops | bytes accessed | tf_op | source)
XLA Modules:
  0.0 501.2 jit_solution(14144372373235077277)
XLA Ops:
  8.0 0.0 copy-start
  8.0 1.3 collective-permute-start
  9.3 4.4 copy.16
  13.7 3.4 reshape_squeeze.3
  17.1 0.0 copy-done
  17.1 0.0 copy-start.8
  17.1 3.3 fusion.156
  20.5 0.0 copy-done.8
  20.5 0.6 fusion.253
  21.7 8.3 %fusion.4 = f32[384,64,52]{0,1,2:T(8,128)S(1)} fusion(f32[384,64,52]{0,2,1:T(8,128)} %fusion.156), kind=kOutput, calls=%fused_computation.7 | convolution fusion | flops 982917120 | bytes 10223616 | tf_op jit(solution)/shard_map/rac,ae->rec/dot_general | solution.py:105
  30.0 5.4 %copy.19 = f32[384,64,52]{0,2,1:T(8,128)} copy(f32[384,64,52]{0,1,2:T(8,128)S(1)} %fusion.4) | data formatting | bytes 10223616 | tf_op jit(solution)/shard_map/rac,ae->rec/transpose | solution.py:105
  35.4 0.0 copy-start.1
  35.4 6.3 %reshape.409 = f32[384,3328]{0,1:T(8,128)} reshape(f32[384,64,52]{0,2,1:T(8,128)} %copy.19) | data formatting | bytes 10223616 | tf_op jit(solution)/shard_map/reshape | solution.py:106
  41.8 0.1 fusion.207
  41.9 0.0 collective-permute-done
  41.9 0.0 copy-done.1
  41.9 0.0 copy-start.3
  41.9 0.3 multiply_reduce_fusion
  42.2 0.6 broadcast_in_dim.8
  42.9 11.6 %all-to-all-start = ((f32[16,1,384]{2,1,0:T(1,128)}), f32[16,1,384]{2,1,0:T(1,128)S(1)}, u32[]{:S(2)}, u32[]{:S(2)}) async-start(f32[16,1,384]{2,1,0:T(1,128)} %broadcast_in_dim.8), calls=%async_computation | async-start | bytes 49152 | tf_op jit(solution)/shard_map/all_to_all | solution.py:24
  54.5 4.5 fusion.3
  59.0 0.0 copy-done.3
  59.0 4.3 all-to-all-done
  63.3 0.0 copy-start.7
  63.3 0.6 copy-done.7
  63.9 4.7 all-to-all-start.1
  69.3 2.1 bitcast_select_fusion
  71.4 0.8 reduce_sum.28
  72.2 64.7 %all-to-all-done.1 = f32[16,384,128]{1,2,0:T(8,128)S(1)} async-done(((f32[16,384,128]{1,2,0:T(8,128)}), f32[16,384,128]{1,2,0:T(8,128)S(1)}, u32[]{:S(2)}, u32[]{:S(2)}) %all-to-all-start.1) | async-done | bytes 3145760 | tf_op jit(solution)/shard_map/all_to_all | solution.py:46
  136.9 0.1 reduce_sum.29
  137.0 0.0 copy-start.2
  137.0 0.0 copy-start.4
  137.0 0.0 copy-start.6
  137.0 1.4 stack.2
  138.4 9.7 %all-to-all-start.2 = ((bf16[16,384,128]{1,2,0:T(8,128)(2,1)}), bf16[16,384,128]{1,2,0:T(8,128)(2,1)S(1)}, u32[]{:S(2)}, u32[]{:S(2)}) async-start(bf16[16,384,128]{1,2,0:T(8,128)(2,1)} %stack.2), calls=%async_computation.3 | async-start | bytes 3145728 | tf_op jit(solution)/shard_map/all_to_all | solution.py:116
  148.1 0.0 all-reduce.7.cloned.1.call-start
  148.2 0.0 copy-done.2
  148.2 0.0 copy-done.4
  148.2 0.0 copy-done.6
  148.2 1.2 broadcast_select_fusion
  149.4 0.0 all-reduce.7.cloned.1.call-update
  149.4 0.0 all-reduce.5.cloned.1.call-start
  149.5 69.4 %all-reduce.7.cloned.1.call-done = (bf16[384,1024]{1,0:T(8,128)(2,1)}, bf16[384,1024]{1,0:T(8,128)(2,1)}) async-done(((bf16[384,1024]{1,0:T(8,128)(2,1)}, bf16[384,1024]{1,0:T(8,128)(2,1)}), (bf16[384,1024]{1,0:T(8,128)(2,1)}, bf16[384,1024]{1,0:T(8,128)(2,1)})) %all-reduce.7.cloned.1.call-update) | async-done | bytes 1572880 | tf_op jit(solution)/shard_map/psum | solution.py:35
  218.8 0.0 all-reduce.5.cloned.1.call-update
  218.9 0.0 reduce-scatter.5.cloned.1.call-start
  218.9 0.0 all-to-all-done.2
  218.9 1.7 fusion.254
  220.6 0.0 reduce-scatter.5.cloned.1.call-update
  220.6 0.0 reduce-scatter.3.cloned.1.call-start
  220.7 90.6 %all-reduce.5.cloned.1.call-done = (bf16[384,1024]{1,0:T(8,128)(2,1)}, bf16[384,1024]{1,0:T(8,128)(2,1)}) async-done(((bf16[384,1024]{1,0:T(8,128)(2,1)}, bf16[384,1024]{1,0:T(8,128)(2,1)}), (bf16[384,1024]{1,0:T(8,128)(2,1)}, bf16[384,1024]{1,0:T(8,128)(2,1)})) %all-reduce.5.cloned.1.call-update) | async-done | bytes 1572880 | tf_op jit(solution)/shard_map/psum | solution.py:35
  311.3 0.0 copy-start.5
  311.3 2.7 convolution_bitcast_fusion
  314.1 0.0 copy-done.5
  314.1 1.4 fusion.252
  315.5 4.1 pad_maximum_fusion
  319.6 0.0 reduce-scatter.3.cloned.1.call-update
  319.6 0.0 reduce-scatter.5.cloned.1.call-done
  319.6 1.6 multiply_bitcast_fusion
  321.2 170.3 %reduce-scatter.3.cloned.1.call-done = f32[2048,128]{1,0:T(8,128)} async-done(((f32[2048,1024]{1,0:T(8,128)}), f32[2048,128]{1,0:T(8,128)}) %reduce-scatter.3.cloned.1.call-update) | async-done | bytes 1048592 | tf_op jit(solution)/shard_map/reduce_scatter | solution.py:52
  491.5 2.3 fusion.8
  (1 shorter events, 0.0 us)
Async XLA Ops:
  8.0 9.1 %copy-start = (bf16[1,52,52]{2,1,0:T(8,128)(2,1)S(1)}, bf16[1,52,52]{2,1,0:T(8,128)(2,1)}, u32[]{:S(2)}) copy-start(bf16[1,52,52]{2,1,0:T(8,128)(2,1)} %param.10) | copy-start | bytes 16228
  8.0 33.9 %collective-permute-start = (bf16[384,1024]{1,0:T(8,128)(2,1)}, bf16[384,1024]{1,0:T(8,128)(2,1)S(1)}, u32[]{:S(2)}, u32[]{:S(2)}) collective-permute-start(bf16[384,1024]{1,0:T(8,128)(2,1)} %bitcast.46), channel_id=1, source_target_pairs={{0,128},{1,129},{2,130},{3,131},{4,132},{5,133},{6,134},{7,135},{8... | collective-permute-start | bytes 2359304 | tf_op jit(solution)/shard_map/ppermute | solution.py:19
  17.1 3.3 copy-start.8
  35.4 6.5 %copy-start.1 = (bf16[1,384,1024]{2,1,0:T(8,128)(2,1)S(1)}, bf16[1,384,1024]{2,1,0:T(8,128)(2,1)}, u32[]{:S(2)}) copy-start(bf16[1,384,1024]{2,1,0:T(8,128)(2,1)} %param.6) | copy-start | bytes 2359300
  41.9 17.1 %copy-start.3 = (bf16[384,1024]{1,0:T(8,128)(2,1)}, bf16[384,1024]{1,0:T(8,128)(2,1)S(1)}, u32[]{:S(2)}) copy-start(bf16[384,1024]{1,0:T(8,128)(2,1)S(1)} %collective-permute-done) | copy-start | bytes 2359300
  42.9 20.4 %all-to-all-start = ((f32[16,1,384]{2,1,0:T(1,128)}), f32[16,1,384]{2,1,0:T(1,128)S(1)}, u32[]{:S(2)}, u32[]{:S(2)}) async-start(f32[16,1,384]{2,1,0:T(1,128)} %broadcast_in_dim.8), calls=%async_computation | async-start | bytes 49152 | tf_op jit(solution)/shard_map/all_to_all | solution.py:24
  63.3 0.6 copy-start.7
  63.9 72.9 %all-to-all-start.1 = ((f32[16,384,128]{1,2,0:T(8,128)}), f32[16,384,128]{1,2,0:T(8,128)S(1)}, u32[]{:S(2)}, u32[]{:S(2)}) async-start(f32[16,384,128]{1,2,0:T(8,128)} %bitcast.13), calls=%async_computation.2 | async-start | bytes 6291456 | tf_op jit(solution)/shard_map/all_to_all | solution.py:46
  137.0 11.2 %copy-start.2 = (bf16[1,384,1024]{2,1,0:T(8,128)(2,1)S(1)}, bf16[1,384,1024]{2,1,0:T(8,128)(2,1)}, u32[]{:S(2)}) copy-start(bf16[1,384,1024]{2,1,0:T(8,128)(2,1)} %param.6) | copy-start | bytes 2359300
  137.0 11.2 %copy-start.4 = (bf16[384,1024]{1,0:T(8,128)(2,1)S(1)}, bf16[384,1024]{1,0:T(8,128)(2,1)}, u32[]{:S(2)}) copy-start(bf16[384,1024]{1,0:T(8,128)(2,1)} %copy-done.3) | copy-start | bytes 2359300
  137.0 11.2 %copy-start.6 = (f32[1,1024]{1,0:T(1,128)S(1)}, f32[1,1024]{1,0:T(1,128)}, u32[]{:S(2)}) copy-start(f32[1,1024]{1,0:T(1,128)} %param.9) | copy-start | bytes 12292
  138.4 80.5 %all-to-all-start.2 = ((bf16[16,384,128]{1,2,0:T(8,128)(2,1)}), bf16[16,384,128]{1,2,0:T(8,128)(2,1)S(1)}, u32[]{:S(2)}, u32[]{:S(2)}) async-start(bf16[16,384,128]{1,2,0:T(8,128)(2,1)} %stack.2), calls=%async_computation.3 | async-start | bytes 3145728 | tf_op jit(solution)/shard_map/all_to_all | solution.py:116
  148.1 70.7 %all-reduce.7.cloned.1.call-start = ((), (), s32[]{:S(2)}) async-start(), calls=%async_computation.8 | async-start | bytes 3145728 | tf_op jit(solution)/shard_map/psum | solution.py:35
  149.4 161.9 %all-reduce.5.cloned.1.call-start = ((), (), s32[]{:S(2)}) async-start(), calls=%async_computation.7 | async-start | bytes 3145728 | tf_op jit(solution)/shard_map/psum | solution.py:35
  218.9 100.8 %reduce-scatter.5.cloned.1.call-start = ((), (), s32[]{:S(2)}) async-start(), calls=%async_computation.6 | async-start | bytes 1179648 | tf_op jit(solution)/shard_map/reduce_scatter | solution.py:123
  220.6 270.9 %reduce-scatter.3.cloned.1.call-start = ((), (), s32[]{:S(2)}) async-start(), calls=%async_computation.5 | async-start | bytes 9437184 | tf_op jit(solution)/shard_map/reduce_scatter | solution.py:52
  311.3 2.7 copy-start.5
Sparse Core Ops, SparseCore 0:
  151.3 67.4 all-reduce.6
  221.5 89.7 all-reduce.4
Sparse Core Ops, SparseCore 1:
  221.9 61.9 reduce-scatter.4
  319.7 171.8 reduce-scatter.2
